TPU v7x, 32 devices: a whole 2x2x4 slice. The times are simulated.
32 devices in a mesh: lat: 8 (over z, y), lon: 4 (over x, core).
Axes of the slice: x: 2, y: 2, z: 4, core: 2. Of those that a mesh axis runs over, the one named last changes fastest.
Arguments:
- pair_table: int32 [640], replicated, may hold values from 0 to 639, each once
- spectral: bfloat16 [640, 384, 1408], P('lat', 'lon'), may hold values from -0.071777344 to 0.071777344
- lat_basis: bfloat16 [640, 32, 1408], P('lat'), may hold values from -0.15625 to 0.15625
- in_weight: bfloat16 [192, 512], replicated, may hold values from -0.4375 to 0.4375
- in_bias: float32 [512], replicated, may hold values from -3 to 3
- out_weight: bfloat16 [512, 192], replicated, may hold values from -0.25 to 0.25
- out_bias: float32 [192], replicated, may hold values from -3 to 3
- cotangent: bfloat16 [64, 192, 2560], P('lat', None, 'lon'), may hold values from -0.08984375 to 0.08984375
Outputs:
- tendency: bfloat16 [64, 192, 2560], P('lat', None, 'lon')
- spectral_grad: bfloat16 [640, 384, 1408], P('lat', 'lon')
- in_weight_grad: float32 [192, 512], replicated
- in_bias_grad: float32 [512], replicated
- out_weight_grad: float32 [512, 192], replicated
- out_bias_grad: float32 [192], replicated
Inputs may be any that keep to these rules, and one draw needn't show every extreme that they name: `pair_table`: each pair number appears exactly once.
All inputs are finite; a program needn't handle non-finite values.
Results may differ from a plain program's by a relative error of at most 0.015.
Values may be sent and summed in bfloat16 or wider, within the bound.
No kernel may reach another device: no remote copies, remote signals or barrier semaphores. Data moves between devices by JAX's collectives and lax.ppermute only.
A program may use at most 256 MiB of HBM per device.

v0:
```python
import math
import jax
import jax.numpy as jnp
from jax import lax
from jax.sharding import PartitionSpec as P

TRUNC = 1279


def pair_masks(pair_ids, length):
    first_len = TRUNC + 1 - pair_ids
    position = jnp.arange(length, dtype=jnp.int32)[None, :]
    lower_part = position < first_len[:, None]
    upper_part = jnp.logical_and(position >= first_len[:, None], position < TRUNC + 2)
    offset = jnp.where(lower_part, position, position - first_len[:, None])
    parity = jnp.where(offset % 2 == 0, 1.0, -1.0).astype(jnp.float32)
    return (lower_part, upper_part, parity, first_len)


def wave_numbers(pair_ids):
    both = jnp.stack([pair_ids, TRUNC - pair_ids], axis=1)
    return both.reshape(-1)


def fourier_table(numbers, longitudes, lon_total):
    phase = numbers[:, None] * longitudes[None, :] % lon_total
    angle = phase.astype(jnp.float32) * (2.0 * math.pi / lon_total)
    factor = jnp.where(numbers == 0, 1.0, 2.0).astype(jnp.float32)[:, None]
    return jnp.stack([factor * jnp.cos(angle), -factor * jnp.sin(angle)], axis=1).astype(
        jnp.bfloat16
    )


def split_parts(coeffs, lower_part, upper_part):
    empty = jnp.zeros_like(coeffs)
    return jnp.stack(
        [
            jnp.where(lower_part[:, None, :], coeffs, empty),
            jnp.where(upper_part[:, None, :], coeffs, empty),
        ],
        axis=1,
    )


def per_device(
    pair_table, spectral, lat_basis, in_weight, in_bias, out_weight, out_bias, cotangent
):
    pair_dev = spectral.shape[0]
    width_local = spectral.shape[1]
    band_rows = cotangent.shape[0]
    block_cols = cotangent.shape[2]
    lon_total = block_cols * lax.axis_size("lon")
    first_row = lax.axis_index("lat") * pair_dev
    local_ids = lax.dynamic_slice_in_dim(pair_table, first_row, pair_dev)
    lower_part, upper_part, parity, first_len = pair_masks(local_ids, spectral.shape[2])
    mirrored = jnp.flip(lat_basis * parity[:, None, :].astype(jnp.bfloat16), axis=1)
    full_basis = jnp.concatenate([lat_basis, mirrored], axis=1)
    lat_window = full_basis.shape[1]
    masked = split_parts(spectral, lower_part, upper_part)
    waves = jnp.einsum(
        "pqkj,plj->pqlk", masked, full_basis, preferred_element_type=jnp.float32
    ).astype(jnp.bfloat16)
    flat_waves = waves.reshape(2 * pair_dev, lat_window * width_local)
    band_waves = lax.all_to_all(flat_waves, "lat", split_axis=1, concat_axis=0, tiled=True)
    wave_count = band_waves.shape[0]
    coeff_grid = band_waves.reshape(wave_count, band_rows, width_local // 2, 2)
    numbers = wave_numbers(pair_table)
    full_table = fourier_table(numbers, jnp.arange(lon_total, dtype=jnp.int32), lon_total)
    all_columns = jnp.einsum(
        "glkc,gcn->lkn", coeff_grid, full_table, preferred_element_type=jnp.float32
    ).astype(jnp.bfloat16)
    grid = lax.all_to_all(all_columns, "lon", split_axis=2, concat_axis=1, tiled=True)
    pre_act = (
        jnp.einsum("lkc,kh->lch", grid, in_weight, preferred_element_type=jnp.float32) + in_bias
    )
    activated, gelu_back = jax.vjp(jax.nn.gelu, pre_act)
    hidden = activated.astype(jnp.bfloat16)
    tendency = (
        jnp.einsum("lch,hk->lkc", hidden, out_weight, preferred_element_type=jnp.float32)
        + out_bias[None, :, None]
    ).astype(jnp.bfloat16)
    out_weight_part = jnp.einsum(
        "lch,lkc->hk", hidden, cotangent, preferred_element_type=jnp.float32
    )
    out_bias_part = jnp.sum(cotangent.astype(jnp.float32), axis=(0, 2))
    hidden_grad = jnp.einsum(
        "lkc,hk->lch", cotangent, out_weight, preferred_element_type=jnp.float32
    )
    pre_grad = gelu_back(hidden_grad)[0].astype(jnp.bfloat16)
    in_weight_part = jnp.einsum("lkc,lch->kh", grid, pre_grad, preferred_element_type=jnp.float32)
    in_bias_part = jnp.sum(pre_grad.astype(jnp.float32), axis=(0, 1))
    grid_grad = jnp.einsum(
        "lch,kh->lkc", pre_grad, in_weight, preferred_element_type=jnp.float32
    ).astype(jnp.bfloat16)
    in_weight_grad, in_bias_grad, out_weight_grad, out_bias_grad = lax.psum(
        (in_weight_part, in_bias_part, out_weight_part, out_bias_part), ("lat", "lon")
    )
    level_rows = lax.all_to_all(grid_grad, "lon", split_axis=1, concat_axis=2, tiled=True)
    wave_grad = jnp.einsum(
        "gcn,lkn->glkc", full_table, level_rows, preferred_element_type=jnp.float32
    ).astype(jnp.bfloat16)
    flat_grad = wave_grad.reshape(wave_count, band_rows * width_local)
    pair_grad = lax.all_to_all(flat_grad, "lat", split_axis=0, concat_axis=1, tiled=True)
    pair_grad = pair_grad.reshape(pair_dev, 2, lat_window, width_local)
    contrib = jnp.einsum(
        "pqlk,plj->pqkj", pair_grad, full_basis, preferred_element_type=jnp.float32
    )
    empty = jnp.zeros_like(contrib[:, 0])
    spectral_grad = (
        jnp.where(lower_part[:, None, :], contrib[:, 0], empty)
        + jnp.where(upper_part[:, None, :], contrib[:, 1], empty)
    ).astype(jnp.bfloat16)
    return (tendency, spectral_grad, in_weight_grad, in_bias_grad, out_weight_grad, out_bias_grad)


def solution(mesh):
    placed = (
        P(),
        P("lat", "lon", None),
        P("lat", None, None),
        P(),
        P(),
        P(),
        P(),
        P("lat", None, "lon"),
    )
    return jax.shard_map(
        per_device,
        mesh=mesh,
        in_specs=placed,
        out_specs=(P("lat", None, "lon"), P("lat", "lon", None), P(), P(), P(), P()),
        check_vma=False,
    )
```

profile of v0, /device:TPU:0, one launch (start us, length us, event | category | flops | bytes accessed | tf_op | source)
XLA Modules:
  0.0 471.3 jit_solution(12344877415564866981)
XLA Ops:
  8.6 7.0 %broadcast_multiply_fusion = bf16[80,32,1408]{2,1,0:T(8,128)(2,1)} fusion(bf16[80,32,1408]{2,1,0:T(8,128)(2,1)} %param.10, bf16[80,1408]{1,0:T(8,128)(2,1)S(1)} %select_convert_fusion), kind=kLoop, calls=%fused_computation.43 | loop fusion | flops 3604480 | bytes 14643200 | tf_op jit(solution)/shard_map/mul | solution.py:56
  15.6 20.3 %rev.4 = bf16[80,32,1408]{2,1,0:T(8,128)(2,1)} reverse(bf16[80,32,1408]{2,1,0:T(8,128)(2,1)} %broadcast_multiply_fusion), dimensions={1} | reverse | bytes 14417920 | tf_op jit(solution)/shard_map/jit(_flip)/rev | solution.py:56
  35.9 23.5 %select_bitcast_fusion.1 = (bf16[80,1,96,1408]{3,2,1,0:T(8,128)(2,1)}, bf16[80,1,96,1408]{3,2,1,0:T(8,128)(2,1)}) fusion(bf16[80,96,1408]{2,1,0:T(8,128)(2,1)} %param.9, pred[80,1408]{1,0:T(8,128)(4,1)S(1)} %get-tuple-element.16, pred[80,1408]{1,0:T(8,128)(4,1)S(1)} %get-tuple-element.17), kind=kLoop, calls=%fused_computation.11 | loop fusion | flops 21626880 | bytes 65105920 | tf_op jit(solution)/shard_map/stack | solution.py:36
  59.4 24.7 %convert_bitcast_fusion = bf16[80,2,64,96]{3,2,1,0:T(8,128)(2,1)} fusion(bf16[80,1,96,1408]{3,2,1,0:T(8,128)(2,1)} %get-tuple-element.11, bf16[80,1,96,1408]{3,2,1,0:T(8,128)(2,1)} %get-tuple-element.10, bf16[80,32,1408]{2,1,0:T(8,128)(2,1)} %rev.4, bf16[80,32,1408]{2,1,0:T(8,128)(2,1)} %param.10), kind=kOutput, calls=%fused_computation.47 | convolution fusion | flops 2884567040 | bytes 59637760 | tf_op jit(solution)/shard_map/pqkj,plj->pqlk/dot_general | solution.py:60
  90.1 7.6 %all-to-all-start = ((bf16[160,8,768]{2,0,1:T(8,128)(2,1)}), bf16[160,8,768]{2,0,1:T(8,128)(2,1)S(1)}, u32[]{:S(2)}, u32[]{:S(2)}) async-start(bf16[160,8,768]{2,0,1:T(8,128)(2,1)} %copy.30), calls=%async_computation | async-start | bytes 3932160 | tf_op jit(solution)/shard_map/all_to_all | solution.py:64
  98.2 58.1 %multiply_convert_fusion.1 = (bf16[1280,1,2560]{2,0,1:T(8,128)(2,1)}, bf16[1280,1,2560]{2,0,1:T(8,128)(2,1)}) fusion(s32[1280]{0:T(1024)S(1)} %reshape.286, f32[1280]{0:T(1024)S(1)} %get-tuple-element.14, f32[1280]{0:T(1024)S(1)} %get-tuple-element.15), kind=kLoop, calls=%fused_computation.23 | loop fusion | flops 42598400 | bytes 13122560 | tf_op jit(solution)/shard_map/convert
  161.6 5.2 %reshape.285 = bf16[1280,8,48,2]{0,3,2,1:T(2,128)(2,1)} reshape(bf16[8,160,768]{1,0,2:T(8,128)(2,1)S(1)} %copy.31) | data formatting | bytes 3932160 | tf_op jit(solution)/shard_map/reshape | solution.py:66
  166.9 9.0 %fusion.26 = bf16[8,48,2560]{2,1,0:T(8,128)(2,1)S(1)} fusion(bf16[1280,1,2560]{2,0,1:T(8,128)(2,1)} %get-tuple-element.13, bf16[1280,1,2560]{2,0,1:T(8,128)(2,1)} %get-tuple-element.12, bf16[1280,8,48,2]{0,3,2,1:T(2,128)(2,1)} %reshape.285), kind=kOutput, calls=%fused_computation.40 | convolution fusion | flops 5040701440 | bytes 17039360 | tf_op jit(solution)/shard_map/glkc,gcn->lkn/dot_general | solution.py:69
  175.9 5.2 %copy.34 = bf16[8,48,2560]{1,0,2:T(8,128)(2,1)} copy(bf16[8,48,2560]{2,1,0:T(8,128)(2,1)S(1)} %fusion.26) | data formatting | bytes 3932160 | tf_op jit(solution)/shard_map/convert_element_type | solution.py:71
  181.1 8.8 %reshape.297 = bf16[4,2,122880]{2,1,0:T(2,128)(2,1)S(1)} reshape(bf16[2560,8,48]{2,1,0:T(8,128)(2,1)} %bitcast.101) | data formatting | bytes 3932160
  190.0 28.0 %all_to_all.68 = bf16[4,2,122880]{2,1,0:T(2,128)(2,1)} all-to-all(bf16[4,2,122880]{2,1,0:T(2,128)(2,1)S(1)} %reshape.297), channel_id=1, replica_groups=mesh['lat'=8,'lon'=4] {'lon'}, dimensions={0} | all-to-all | bytes 3932160 | tf_op jit(solution)/shard_map/all_to_all | solution.py:72
  218.0 7.0 %reshape.298 = bf16[2560,8,48]{2,1,0:T(8,128)(2,1)} reshape(bf16[4,2,122880]{2,1,0:T(2,128)(2,1)} %all_to_all.68) | data formatting | bytes 3932160
  225.0 5.7 %copy.35 = bf16[8,48,4,640]{3,1,2,0:T(8,128)(2,1)S(1)} copy(bf16[8,48,4,640]{1,0,3,2:T(8,128)(2,1)} %bitcast.102) | data formatting | bytes 3932160 | tf_op jit(solution)/shard_map/all_to_all | solution.py:72
  230.8 5.5 %multiply_convert_fusion.2 = (bf16[8,640,512]{2,1,0:T(8,128)(2,1)}, f32[8,640,512]{2,1,0:T(8,128)S(1)}) fusion(f32[512]{0:T(512)S(1)} %copy-done.13, bf16[8,192,640]{2,1,0:T(8,128)(2,1)S(1)} %bitcast.107, bf16[192,512]{1,0:T(8,128)(2,1)S(1)} %copy-done), kind=kOutput, calls=%fused_computation.36 | convolution fusion | flops 1032847360 | bytes 17893376 | tf_op jit(solution)/shard_map/lkc,kh->lch/dot_general | solution.py:74
  236.3 8.7 %convert_reduce_fusion = (f32[512]{0:T(512)S(1)}, bf16[8,640,512]{2,1,0:T(8,128)(2,1)S(1)}) fusion(f32[8,640,512]{2,1,0:T(8,128)S(1)} %get-tuple-element.19, f32[512]{0:T(512)S(1)} %copy-done.13, bf16[8,192,640]{2,1,0:T(8,128)(2,1)S(1)} %copy-done.4, bf16[512,192]{0,1:T(8,128)(2,1)S(1)} %copy-done.12), kind=kOutput, calls=%fused_computation.35 | convolution fusion | flops 1066925568 | bytes 17895424 | tf_op jit(solution)/shard_map/lkc,hk->lch/dot_general | solution.py:86
  248.0 26.9 %all_to_all.69 = bf16[8,192,640]{2,0,1:T(8,128)(2,1)S(1)} all-to-all(bf16[8,192,640]{2,0,1:T(8,128)(2,1)S(1)} %copy.36), channel_id=1, replica_groups=mesh['lat'=8,'lon'=4] {'lon'}, dimensions={1} | all-to-all | bytes 3932160 | tf_op jit(solution)/shard_map/all_to_all | solution.py:98
  278.6 9.0 %fusion.28 = bf16[1280,8,48,2]{0,2,3,1:T(8,128)(2,1)S(1)} fusion(bf16[1280,1,2560]{2,0,1:T(8,128)(2,1)} %get-tuple-element.13, bf16[1280,1,2560]{2,0,1:T(8,128)(2,1)} %get-tuple-element.12, bf16[8,48,2560,1]{2,1,0,3:T(8,128)(2,1)} %reshape.293), kind=kOutput, calls=%fused_computation.45 | convolution fusion | flops 5060362240 | bytes 17039360 | tf_op jit(solution)/shard_map/gcn,lkn->glkc/dot_general | solution.py:99
  290.4 6.4 %all_to_all.61 = bf16[8,160,768]{1,0,2:T(8,128)(2,1)S(1)} reshape(bf16[1280,8,48,2]{0,3,2,1:T(2,128)(2,1)} %copy.38) | data formatting | bytes 3932160 | tf_op jit(solution)/shard_map/all_to_all | solution.py:103
  300.1 6.0 %all-to-all-start.3 = ((bf16[8,160,768]{2,1,0:T(8,128)(2,1)}), bf16[8,160,768]{2,1,0:T(8,128)(2,1)S(1)}, u32[]{:S(2)}, u32[]{:S(2)}) async-start(bf16[8,160,768]{2,1,0:T(8,128)(2,1)} %copy.39), calls=%async_computation.3 | async-start | bytes 3932160 | tf_op jit(solution)/shard_map/all_to_all | solution.py:103
  308.2 5.0 %convolution_bitcast_fusion.1 = f32[192,512]{1,0:T(8,128)} fusion(bf16[8,192,640]{2,1,0:T(8,128)(2,1)} %bitcast.108, bf16[8,640,512]{2,1,0:T(8,128)(2,1)} %copy-done.3), kind=kOutput, calls=%fused_computation.54 | convolution fusion | flops 1006632960 | bytes 7602176 | tf_op jit(solution)/shard_map/lkc,lch->kh/dot_general | solution.py:90
  317.7 56.7 %all-reduce = (f32[512]{0:T(512)}, f32[192]{0:T(256)}) all-reduce(f32[512]{0:T(512)S(1)} %get-tuple-element.20, f32[192]{0:T(256)S(1)} %convert_reduce_fusion.1), channel_id=1, replica_groups=mesh['lat'=8,'lon'=4] {'lat','lon'}, use_global_device_ids=true, to_apply=%region_2.3 | all-reduce | flops 704 | bytes 5632 | tf_op jit(solution)/shard_map/psum | solution.py:95
  374.4 5.7 %fusion.36 = bf16[8,192,640]{2,1,0:T(8,128)(2,1)} fusion(f32[192]{0:T(256)S(1)} %copy-done.14, bf16[8,640,512]{2,1,0:T(8,128)(2,1)} %get-tuple-element.18, bf16[512,192]{0,1:T(8,128)(2,1)S(1)} %copy-done.12), kind=kOutput, calls=%fused_computation.52 | convolution fusion | flops 1008599040 | bytes 7406336 | tf_op jit(solution)/shard_map/lch,hk->lkc/dot_general | solution.py:79
  387.0 34.6 %fusion.9 = f32[80,2,96,1408]{3,2,0,1:T(8,128)} fusion(bf16[80,32,1408]{2,1,0:T(8,128)(2,1)} %rev.4, bf16[80,32,1408]{2,1,0:T(8,128)(2,1)} %param.10, bf16[80,2,64,96]{3,2,1,0:T(8,128)(2,1)S(1)} %reshape.287), kind=kOutput, calls=%fused_computation.17 | convolution fusion | flops 2797076480 | bytes 102891520 | tf_op jit(solution)/shard_map/pqlk,plj->pqkj/dot_general | solution.py:105
  421.6 36.2 %fusion.2 = bf16[80,96,1408]{2,1,0:T(8,128)(2,1)} fusion(f32[80,2,96,1408]{3,2,0,1:T(8,128)} %fusion.9, pred[80,1408]{1,0:T(8,128)(4,1)S(1)} %copy-done.10, pred[80,1408]{1,0:T(8,128)(4,1)S(1)} %copy-done.8), kind=kLoop, calls=%fused_computation.3 | loop fusion | flops 43253760 | bytes 108359680 | tf_op jit(solution)/shard_map/convert_element_type | solution.py:112
  (61 shorter events, 45.7 us)
Async XLA Ops:
  7.2 223.6 %copy-start = (bf16[192,512]{1,0:T(8,128)(2,1)S(1)}, bf16[192,512]{1,0:T(8,128)(2,1)}, u32[]{:S(2)}) copy-start(bf16[192,512]{1,0:T(8,128)(2,1)} %param.11) | copy-start | bytes 589828
  8.6 27.4 %copy-start.7 = (pred[80,1408]{1,0:T(8,128)(4,1)}, pred[80,1408]{1,0:T(8,128)(4,1)S(1)}, u32[]{:S(2)}) copy-start(pred[80,1408]{1,0:T(8,128)(4,1)S(1)} %get-tuple-element.16) | copy-start | bytes 337924
  8.6 27.4 %copy-start.9 = (pred[80,1408]{1,0:T(8,128)(4,1)}, pred[80,1408]{1,0:T(8,128)(4,1)S(1)}, u32[]{:S(2)}) copy-start(pred[80,1408]{1,0:T(8,128)(4,1)S(1)} %get-tuple-element.17) | copy-start | bytes 337924
  84.1 13.6 %copy-start.11 = (s32[640]{0:T(1024)S(1)}, s32[640]{0:T(1024)}, u32[]{:S(2)}) copy-start(s32[640]{0:T(1024)} %param.8) | copy-start | bytes 7684
  90.1 66.2 %all-to-all-start = ((bf16[160,8,768]{2,0,1:T(8,128)(2,1)}), bf16[160,8,768]{2,0,1:T(8,128)(2,1)S(1)}, u32[]{:S(2)}, u32[]{:S(2)}) async-start(bf16[160,8,768]{2,0,1:T(8,128)(2,1)} %copy.30), calls=%async_computation | async-start | bytes 3932160 | tf_op jit(solution)/shard_map/all_to_all | solution.py:64
  156.3 1.3 copy-start.2
  189.9 40.8 %copy-start.13 = (f32[512]{0:T(512)S(1)}, f32[512]{0:T(512)}, u32[]{:S(2)}) copy-start(f32[512]{0:T(512)} %param.12) | copy-start | bytes 6148
  230.8 5.5 %copy-start.6 = (bf16[8,48,4,640]{3,1,2,0:T(8,128)(2,1)}, bf16[8,48,4,640]{3,1,2,0:T(8,128)(2,1)S(1)}, u32[]{:S(2)}) copy-start(bf16[8,48,4,640]{3,1,2,0:T(8,128)(2,1)S(1)} %copy.35) | copy-start | bytes 5898244
  230.8 5.5 %copy-start.4 = (bf16[8,192,640]{2,1,0:T(8,128)(2,1)S(1)}, bf16[8,192,640]{2,1,0:T(8,128)(2,1)}, u32[]{:S(2)}) copy-start(bf16[8,192,640]{2,1,0:T(8,128)(2,1)} %param.15) | copy-start | bytes 5898244
  230.8 5.5 %copy-start.12 = (bf16[512,192]{0,1:T(8,128)(2,1)S(1)}, bf16[512,192]{0,1:T(8,128)(2,1)}, u32[]{:S(2)}) copy-start(bf16[512,192]{0,1:T(8,128)(2,1)} %param.13) | copy-start | bytes 589828
  245.0 31.4 %copy-start.3 = (bf16[8,640,512]{2,1,0:T(8,128)(2,1)}, bf16[8,640,512]{2,1,0:T(8,128)(2,1)S(1)}, u32[]{:S(2)}) copy-start(bf16[8,640,512]{2,1,0:T(8,128)(2,1)S(1)} %get-tuple-element.21) | copy-start | bytes 15728644
  300.1 80.0 %all-to-all-start.3 = ((bf16[8,160,768]{2,1,0:T(8,128)(2,1)}), bf16[8,160,768]{2,1,0:T(8,128)(2,1)S(1)}, u32[]{:S(2)}, u32[]{:S(2)}) async-start(bf16[8,160,768]{2,1,0:T(8,128)(2,1)} %copy.39), calls=%async_computation.3 | async-start | bytes 3932160 | tf_op jit(solution)/shard_map/all_to_all | solution.py:103
  306.1 154.6 %all-reduce.4.cloned.1.call-start = ((), (), s32[]{:S(2)}) async-start(), calls=%async_computation.4 | async-start | bytes 1572864 | tf_op jit(solution)/shard_map/psum | solution.py:95
  306.1 7.1 %copy-start.5 = (bf16[8,192,640]{2,1,0:T(8,128)(2,1)S(1)}, bf16[8,192,640]{2,1,0:T(8,128)(2,1)}, u32[]{:S(2)}) copy-start(bf16[8,192,640]{2,1,0:T(8,128)(2,1)} %param.15) | copy-start | bytes 5898244
  308.2 66.2 %copy-start.14 = (f32[192]{0:T(256)S(1)}, f32[192]{0:T(256)}, u32[]{:S(2)}) copy-start(f32[192]{0:T(256)} %param.14) | copy-start | bytes 2308
  387.0 34.6 %copy-start.8 = (pred[80,1408]{1,0:T(8,128)(4,1)S(1)}, pred[80,1408]{1,0:T(8,128)(4,1)}, u32[]{:S(2)}) copy-start(pred[80,1408]{1,0:T(8,128)(4,1)} %copy-done.7) | copy-start | bytes 337924
  387.0 34.6 %copy-start.10 = (pred[80,1408]{1,0:T(8,128)(4,1)S(1)}, pred[80,1408]{1,0:T(8,128)(4,1)}, u32[]{:S(2)}) copy-start(pred[80,1408]{1,0:T(8,128)(4,1)} %copy-done.9) | copy-start | bytes 337924
  421.6 42.6 %copy-start.1 = (bf16[192,512]{1,0:T(8,128)(2,1)S(1)}, bf16[192,512]{1,0:T(8,128)(2,1)}, u32[]{:S(2)}) copy-start(bf16[192,512]{1,0:T(8,128)(2,1)} %param.11) | copy-start | bytes 589828
Sparse Core Ops, SparseCore 0:
  317.8 142.8 all-reduce.3
where the time goes:
time: 477 us; the launch traced here: 471 us
  other arithmetic  128 us (27%)
  blocking collectives  112 us (23%)
  matrix products  108 us (23%)
  local copies, waits for them, and re-layouts  91.9 us (19%)
  between operations  14.6 us (3%)
  starting transfers between devices  13.6 us (3%)
    another operation x1, other arithmetic  58.1 us
    psum x1, blocking collectives, per_device(): lax.psum((in_weight_part, in_bias_part, out_weight_part, out_bias_part),...  56.7 us
    convert_element_type x1, other arithmetic, per_device(): spectral_grad = (jnp.where(lower_part[:, None, :], contrib[:, 0], empty)...  36.2 us
    dot_general x1, matrix products, per_device(): jnp.einsum('pqlk,plj->pqkj', pair_grad, full_basis, preferred_element_typ...  34.6 us
    all_to_all x1, blocking collectives, per_device(): lax.all_to_all(all_columns, 'lon', split_axis=2, concat_axis=1, tiled=True)  28 us
    all_to_all x1, blocking collectives, per_device(): lax.all_to_all(grid_grad, 'lon', split_axis=1, concat_axis=2, tiled=True)  26.9 us
    dot_general x1, matrix products, per_device(): jnp.einsum('pqkj,plj->pqlk', masked, full_basis, preferred_element_type=j...  24.7 us
    another operation x1, other arithmetic, split_parts(): jnp.stack([jnp.where(lower_part[:, None, :], coeffs, empty), jnp.where(up...  23.5 us
  transfers between devices with their start and end apart: 3, of which 1 were waited for; matrix products, arithmetic and copies ran while one was open for 33% of the time, Pallas kernels for 0%

commit v1 on v0

--- a/solution.py
+++ b/solution.py
@@ -92,8 +92,11 @@
     grid_grad = jnp.einsum(
         "lch,kh->lkc", pre_grad, in_weight, preferred_element_type=jnp.float32
     ).astype(jnp.bfloat16)
-    in_weight_grad, in_bias_grad, out_weight_grad, out_bias_grad = lax.psum(
-        (in_weight_part, in_bias_part, out_weight_part, out_bias_part), ("lat", "lon")
+    close_bench = lambda row_data, mesh_name, comm_axis: lax.psum(
+        lax.psum(row_data, mesh_name), comm_axis
+    )
+    in_weight_grad, in_bias_grad, out_weight_grad, out_bias_grad = close_bench(
+        (in_weight_part, in_bias_part, out_weight_part, out_bias_part), "lon", "lat"
     )
     level_rows = lax.all_to_all(grid_grad, "lon", split_axis=1, concat_axis=2, tiled=True)
     wave_grad = jnp.einsum(

time: 477 us -> 458 us (0.960)
  blocking collectives: 112 us -> 91 us
    psum x1 -> x2, blocking collectives: 56.7 us -> 36 us  [the longest x1 30 us: per_device(): lax.psum(lax.psum(row_data, mesh_name), comm_axis)]
  transfers between devices with their start and end apart: 3 -> 4, of which waited for: 1 -> 1; matrix products, arithmetic and copies ran while one was open for 33% -> 34% of each run, Pallas kernels for 0% -> 0%
where the time goes in v1:
time: 458 us; the launch traced here: 450 us
  other arithmetic  128 us (28%)
  matrix products  108 us (24%)
  local copies, waits for them, and re-layouts  91.9 us (20%)
  blocking collectives  91 us (20%)
  between operations  14.6 us (3%)
  starting transfers between devices  13.7 us (3%)
    another operation x1, other arithmetic  58.1 us
    convert_element_type x1, other arithmetic, per_device(): spectral_grad = (jnp.where(lower_part[:, None, :], contrib[:, 0], empty)...  36.3 us
    dot_general x1, matrix products, per_device(): jnp.einsum('pqlk,plj->pqkj', pair_grad, full_basis, preferred_element_typ...  34.7 us
    psum x1, blocking collectives, per_device(): lax.psum(lax.psum(row_data, mesh_name), comm_axis)  30 us
    all_to_all x1, blocking collectives, per_device(): lax.all_to_all(all_columns, 'lon', split_axis=2, concat_axis=1, tiled=True)  28 us
    all_to_all x1, blocking collectives, per_device(): lax.all_to_all(grid_grad, 'lon', split_axis=1, concat_axis=2, tiled=True)  26.9 us
    dot_general x1, matrix products, per_device(): jnp.einsum('pqkj,plj->pqlk', masked, full_basis, preferred_element_type=j...  24.7 us
    another operation x1, other arithmetic, split_parts(): jnp.stack([jnp.where(lower_part[:, None, :], coeffs, empty), jnp.where(up...  23.5 us
  transfers between devices with their start and end apart: 4, of which 1 were waited for; matrix products, arithmetic and copies ran while one was open for 34% of the time, Pallas kernels for 0%

profile of v1, /device:TPU:0, one launch (start us, length us, event | category | flops | bytes accessed | tf_op | source)
XLA Modules:
  0.0 449.7 jit_solution(7989691860063467664)
XLA Ops:
  8.6 7.0 %broadcast_multiply_fusion = bf16[80,32,1408]{2,1,0:T(8,128)(2,1)} fusion(bf16[80,32,1408]{2,1,0:T(8,128)(2,1)} %param.10, bf16[80,1408]{1,0:T(8,128)(2,1)S(1)} %select_convert_fusion), kind=kLoop, calls=%fused_computation.43 | loop fusion | flops 3604480 | bytes 14643200 | tf_op jit(solution)/shard_map/mul | solution.py:56
  15.6 20.3 %rev.4 = bf16[80,32,1408]{2,1,0:T(8,128)(2,1)} reverse(bf16[80,32,1408]{2,1,0:T(8,128)(2,1)} %broadcast_multiply_fusion), dimensions={1} | reverse | bytes 14417920 | tf_op jit(solution)/shard_map/jit(_flip)/rev | solution.py:56
  35.9 23.5 %select_bitcast_fusion.1 = (bf16[80,1,96,1408]{3,2,1,0:T(8,128)(2,1)}, bf16[80,1,96,1408]{3,2,1,0:T(8,128)(2,1)}) fusion(bf16[80,96,1408]{2,1,0:T(8,128)(2,1)} %param.9, pred[80,1408]{1,0:T(8,128)(4,1)S(1)} %get-tuple-element.20, pred[80,1408]{1,0:T(8,128)(4,1)S(1)} %get-tuple-element.21), kind=kLoop, calls=%fused_computation.11 | loop fusion | flops 21626880 | bytes 65105920 | tf_op jit(solution)/shard_map/stack | solution.py:36
  59.4 24.7 %convert_bitcast_fusion = bf16[80,2,64,96]{3,2,1,0:T(8,128)(2,1)} fusion(bf16[80,1,96,1408]{3,2,1,0:T(8,128)(2,1)} %get-tuple-element.15, bf16[80,1,96,1408]{3,2,1,0:T(8,128)(2,1)} %get-tuple-element.14, bf16[80,32,1408]{2,1,0:T(8,128)(2,1)} %rev.4, bf16[80,32,1408]{2,1,0:T(8,128)(2,1)} %param.10), kind=kOutput, calls=%fused_computation.47 | convolution fusion | flops 2884567040 | bytes 59637760 | tf_op jit(solution)/shard_map/pqkj,plj->pqlk/dot_general | solution.py:60
  90.1 7.6 %all-to-all-start = ((bf16[160,8,768]{2,0,1:T(8,128)(2,1)}), bf16[160,8,768]{2,0,1:T(8,128)(2,1)S(1)}, u32[]{:S(2)}, u32[]{:S(2)}) async-start(bf16[160,8,768]{2,0,1:T(8,128)(2,1)} %copy.30), calls=%async_computation | async-start | bytes 3932160 | tf_op jit(solution)/shard_map/all_to_all | solution.py:64
  98.2 58.1 %multiply_convert_fusion.1 = (bf16[1280,1,2560]{2,0,1:T(8,128)(2,1)}, bf16[1280,1,2560]{2,0,1:T(8,128)(2,1)}) fusion(s32[1280]{0:T(1024)S(1)} %reshape.286, f32[1280]{0:T(1024)S(1)} %get-tuple-element.18, f32[1280]{0:T(1024)S(1)} %get-tuple-element.19), kind=kLoop, calls=%fused_computation.23 | loop fusion | flops 42598400 | bytes 13122560 | tf_op jit(solution)/shard_map/convert
  161.6 5.2 %reshape.285 = bf16[1280,8,48,2]{0,3,2,1:T(2,128)(2,1)} reshape(bf16[8,160,768]{1,0,2:T(8,128)(2,1)S(1)} %copy.31) | data formatting | bytes 3932160 | tf_op jit(solution)/shard_map/reshape | solution.py:66
  166.9 9.0 %fusion.26 = bf16[8,48,2560]{2,1,0:T(8,128)(2,1)S(1)} fusion(bf16[1280,1,2560]{2,0,1:T(8,128)(2,1)} %get-tuple-element.17, bf16[1280,1,2560]{2,0,1:T(8,128)(2,1)} %get-tuple-element.16, bf16[1280,8,48,2]{0,3,2,1:T(2,128)(2,1)} %reshape.285), kind=kOutput, calls=%fused_computation.40 | convolution fusion | flops 5040701440 | bytes 17039360 | tf_op jit(solution)/shard_map/glkc,gcn->lkn/dot_general | solution.py:69
  175.9 5.2 %copy.34 = bf16[8,48,2560]{1,0,2:T(8,128)(2,1)} copy(bf16[8,48,2560]{2,1,0:T(8,128)(2,1)S(1)} %fusion.26) | data formatting | bytes 3932160 | tf_op jit(solution)/shard_map/convert_element_type | solution.py:71
  181.1 8.8 %reshape.297 = bf16[4,2,122880]{2,1,0:T(2,128)(2,1)S(1)} reshape(bf16[2560,8,48]{2,1,0:T(8,128)(2,1)} %bitcast.101) | data formatting | bytes 3932160
  190.0 28.0 %all_to_all.68 = bf16[4,2,122880]{2,1,0:T(2,128)(2,1)} all-to-all(bf16[4,2,122880]{2,1,0:T(2,128)(2,1)S(1)} %reshape.297), channel_id=1, replica_groups=mesh['lat'=8,'lon'=4] {'lon'}, dimensions={0} | all-to-all | bytes 3932160 | tf_op jit(solution)/shard_map/all_to_all | solution.py:72
  218.0 7.0 %reshape.298 = bf16[2560,8,48]{2,1,0:T(8,128)(2,1)} reshape(bf16[4,2,122880]{2,1,0:T(2,128)(2,1)} %all_to_all.68) | data formatting | bytes 3932160
  225.0 5.7 %copy.35 = bf16[8,48,4,640]{3,1,2,0:T(8,128)(2,1)S(1)} copy(bf16[8,48,4,640]{1,0,3,2:T(8,128)(2,1)} %bitcast.102) | data formatting | bytes 3932160 | tf_op jit(solution)/shard_map/all_to_all | solution.py:72
  230.8 5.5 %multiply_convert_fusion.2 = (bf16[8,640,512]{2,1,0:T(8,128)(2,1)}, f32[8,640,512]{2,1,0:T(8,128)S(1)}) fusion(f32[512]{0:T(512)S(1)} %copy-done.13, bf16[8,192,640]{2,1,0:T(8,128)(2,1)S(1)} %bitcast.107, bf16[192,512]{1,0:T(8,128)(2,1)S(1)} %copy-done), kind=kOutput, calls=%fused_computation.36 | convolution fusion | flops 1032847360 | bytes 17893376 | tf_op jit(solution)/shard_map/lkc,kh->lch/dot_general | solution.py:74
  236.3 8.7 %convert_reduce_fusion = (f32[512]{0:T(512)S(1)}, bf16[8,640,512]{2,1,0:T(8,128)(2,1)S(1)}) fusion(f32[8,640,512]{2,1,0:T(8,128)S(1)} %get-tuple-element.23, f32[512]{0:T(512)S(1)} %copy-done.13, bf16[8,192,640]{2,1,0:T(8,128)(2,1)S(1)} %copy-done.4, bf16[512,192]{0,1:T(8,128)(2,1)S(1)} %copy-done.12), kind=kOutput, calls=%fused_computation.35 | convolution fusion | flops 1066925568 | bytes 17895424 | tf_op jit(solution)/shard_map/lkc,hk->lch/dot_general | solution.py:86
  248.0 26.9 %all_to_all.69 = bf16[8,192,640]{2,0,1:T(8,128)(2,1)S(1)} all-to-all(bf16[8,192,640]{2,0,1:T(8,128)(2,1)S(1)} %copy.36), channel_id=1, replica_groups=mesh['lat'=8,'lon'=4] {'lon'}, dimensions={1} | all-to-all | bytes 3932160 | tf_op jit(solution)/shard_map/all_to_all | solution.py:101
  278.6 9.0 %fusion.28 = bf16[1280,8,48,2]{0,2,3,1:T(8,128)(2,1)S(1)} fusion(bf16[1280,1,2560]{2,0,1:T(8,128)(2,1)} %get-tuple-element.17, bf16[1280,1,2560]{2,0,1:T(8,128)(2,1)} %get-tuple-element.16, bf16[8,48,2560,1]{2,1,0,3:T(8,128)(2,1)} %reshape.293), kind=kOutput, calls=%fused_computation.45 | convolution fusion | flops 5060362240 | bytes 17039360 | tf_op jit(solution)/shard_map/gcn,lkn->glkc/dot_general | solution.py:102
  290.4 6.4 %all_to_all.61 = bf16[8,160,768]{1,0,2:T(8,128)(2,1)S(1)} reshape(bf16[1280,8,48,2]{0,3,2,1:T(2,128)(2,1)} %copy.38) | data formatting | bytes 3932160 | tf_op jit(solution)/shard_map/all_to_all | solution.py:106
  300.1 6.0 %all-to-all-start.3 = ((bf16[8,160,768]{2,1,0:T(8,128)(2,1)}), bf16[8,160,768]{2,1,0:T(8,128)(2,1)S(1)}, u32[]{:S(2)}, u32[]{:S(2)}) async-start(bf16[8,160,768]{2,1,0:T(8,128)(2,1)} %copy.39), calls=%async_computation.3 | async-start | bytes 3932160 | tf_op jit(solution)/shard_map/all_to_all | solution.py:106
  317.7 6.0 %all-reduce.2 = (f32[512]{0:T(512)S(1)}, f32[192]{0:T(256)S(1)}) all-reduce(f32[512]{0:T(512)S(1)} %get-tuple-element.24, f32[192]{0:T(256)S(1)} %convert_reduce_fusion.1), channel_id=1, replica_groups=mesh['lat'=8,'lon'=4] {'lon'}, use_global_device_ids=true, to_apply=%region_3.4 | all-reduce | flops 704 | bytes 5632 | tf_op jit(solution)/shard_map/psum | solution.py:96
  323.7 30.0 %all-reduce = (f32[512]{0:T(512)}, f32[192]{0:T(256)}) all-reduce(f32[512]{0:T(512)S(1)} %get-tuple-element.10, f32[192]{0:T(256)S(1)} %get-tuple-element.11), channel_id=1, replica_groups=mesh['lat'=8,'lon'=4] {'lat'}, use_global_device_ids=true, to_apply=%region_4.5 | all-reduce | flops 704 | bytes 5632 | tf_op jit(solution)/shard_map/psum | solution.py:95
  353.7 5.6 %fusion.36 = bf16[8,192,640]{2,1,0:T(8,128)(2,1)} fusion(f32[192]{0:T(256)S(1)} %copy-done.14, bf16[8,640,512]{2,1,0:T(8,128)(2,1)} %get-tuple-element.22, bf16[512,192]{0,1:T(8,128)(2,1)S(1)} %copy-done.12), kind=kOutput, calls=%fused_computation.52 | convolution fusion | flops 1008599040 | bytes 7406336 | tf_op jit(solution)/shard_map/lch,hk->lkc/dot_general | solution.py:79
  366.3 34.7 %fusion.9 = f32[80,2,96,1408]{3,2,0,1:T(8,128)} fusion(bf16[80,32,1408]{2,1,0:T(8,128)(2,1)} %rev.4, bf16[80,32,1408]{2,1,0:T(8,128)(2,1)} %param.10, bf16[80,2,64,96]{3,2,1,0:T(8,128)(2,1)S(1)} %reshape.287), kind=kOutput, calls=%fused_computation.17 | convolution fusion | flops 2797076480 | bytes 102891520 | tf_op jit(solution)/shard_map/pqlk,plj->pqkj/dot_general | solution.py:108
  401.1 36.3 %fusion.2 = bf16[80,96,1408]{2,1,0:T(8,128)(2,1)} fusion(f32[80,2,96,1408]{3,2,0,1:T(8,128)} %fusion.9, pred[80,1408]{1,0:T(8,128)(4,1)S(1)} %copy-done.10, pred[80,1408]{1,0:T(8,128)(4,1)S(1)} %copy-done.8), kind=kLoop, calls=%fused_computation.3 | loop fusion | flops 43253760 | bytes 108359680 | tf_op jit(solution)/shard_map/convert_element_type | solution.py:115
  (65 shorter events, 49.6 us)
Async XLA Ops:
  7.2 223.6 %copy-start = (bf16[192,512]{1,0:T(8,128)(2,1)S(1)}, bf16[192,512]{1,0:T(8,128)(2,1)}, u32[]{:S(2)}) copy-start(bf16[192,512]{1,0:T(8,128)(2,1)} %param.11) | copy-start | bytes 589828
  8.6 27.4 %copy-start.7 = (pred[80,1408]{1,0:T(8,128)(4,1)}, pred[80,1408]{1,0:T(8,128)(4,1)S(1)}, u32[]{:S(2)}) copy-start(pred[80,1408]{1,0:T(8,128)(4,1)S(1)} %get-tuple-element.20) | copy-start | bytes 337924
  8.6 27.4 %copy-start.9 = (pred[80,1408]{1,0:T(8,128)(4,1)}, pred[80,1408]{1,0:T(8,128)(4,1)S(1)}, u32[]{:S(2)}) copy-start(pred[80,1408]{1,0:T(8,128)(4,1)S(1)} %get-tuple-element.21) | copy-start | bytes 337924
  84.1 13.6 %copy-start.11 = (s32[640]{0:T(1024)S(1)}, s32[640]{0:T(1024)}, u32[]{:S(2)}) copy-start(s32[640]{0:T(1024)} %param.8) | copy-start | bytes 7684
  90.1 66.2 %all-to-all-start = ((bf16[160,8,768]{2,0,1:T(8,128)(2,1)}), bf16[160,8,768]{2,0,1:T(8,128)(2,1)S(1)}, u32[]{:S(2)}, u32[]{:S(2)}) async-start(bf16[160,8,768]{2,0,1:T(8,128)(2,1)} %copy.30), calls=%async_computation | async-start | bytes 3932160 | tf_op jit(solution)/shard_map/all_to_all | solution.py:64
  156.3 1.3 copy-start.2
  189.9 40.8 %copy-start.13 = (f32[512]{0:T(512)S(1)}, f32[512]{0:T(512)}, u32[]{:S(2)}) copy-start(f32[512]{0:T(512)} %param.12) | copy-start | bytes 6148
  230.8 5.5 %copy-start.6 = (bf16[8,48,4,640]{3,1,2,0:T(8,128)(2,1)}, bf16[8,48,4,640]{3,1,2,0:T(8,128)(2,1)S(1)}, u32[]{:S(2)}) copy-start(bf16[8,48,4,640]{3,1,2,0:T(8,128)(2,1)S(1)} %copy.35) | copy-start | bytes 5898244
  230.8 5.5 %copy-start.4 = (bf16[8,192,640]{2,1,0:T(8,128)(2,1)S(1)}, bf16[8,192,640]{2,1,0:T(8,128)(2,1)}, u32[]{:S(2)}) copy-start(bf16[8,192,640]{2,1,0:T(8,128)(2,1)} %param.15) | copy-start | bytes 5898244
  230.8 5.5 %copy-start.12 = (bf16[512,192]{0,1:T(8,128)(2,1)S(1)}, bf16[512,192]{0,1:T(8,128)(2,1)}, u32[]{:S(2)}) copy-start(bf16[512,192]{0,1:T(8,128)(2,1)} %param.13) | copy-start | bytes 589828
  245.0 31.4 %copy-start.3 = (bf16[8,640,512]{2,1,0:T(8,128)(2,1)}, bf16[8,640,512]{2,1,0:T(8,128)(2,1)S(1)}, u32[]{:S(2)}) copy-start(bf16[8,640,512]{2,1,0:T(8,128)(2,1)S(1)} %get-tuple-element.25) | copy-start | bytes 15728644
  300.1 59.3 %all-to-all-start.3 = ((bf16[8,160,768]{2,1,0:T(8,128)(2,1)}), bf16[8,160,768]{2,1,0:T(8,128)(2,1)S(1)}, u32[]{:S(2)}, u32[]{:S(2)}) async-start(bf16[8,160,768]{2,1,0:T(8,128)(2,1)} %copy.39), calls=%async_computation.3 | async-start | bytes 3932160 | tf_op jit(solution)/shard_map/all_to_all | solution.py:106
  306.1 53.3 %all-reduce.9.cloned.1.call-start = ((), (), s32[]{:S(2)}) async-start(), calls=%async_computation.5 | async-start | bytes 1572864 | tf_op jit(solution)/shard_map/psum | solution.py:96
  306.1 7.1 %copy-start.5 = (bf16[8,192,640]{2,1,0:T(8,128)(2,1)S(1)}, bf16[8,192,640]{2,1,0:T(8,128)(2,1)}, u32[]{:S(2)}) copy-start(bf16[8,192,640]{2,1,0:T(8,128)(2,1)} %param.15) | copy-start | bytes 5898244
  308.2 45.5 %copy-start.14 = (f32[192]{0:T(256)S(1)}, f32[192]{0:T(256)}, u32[]{:S(2)}) copy-start(f32[192]{0:T(256)} %param.14) | copy-start | bytes 2308
  317.7 121.5 %all-reduce.7.cloned.1.call-start = ((), (), s32[]{:S(2)}) async-start(), calls=%async_computation.4 | async-start | bytes 1572864 | tf_op jit(solution)/shard_map/psum | solution.py:95
  366.3 34.8 %copy-start.8 = (pred[80,1408]{1,0:T(8,128)(4,1)S(1)}, pred[80,1408]{1,0:T(8,128)(4,1)}, u32[]{:S(2)}) copy-start(pred[80,1408]{1,0:T(8,128)(4,1)} %copy-done.7) | copy-start | bytes 337924
  366.3 34.8 %copy-start.10 = (pred[80,1408]{1,0:T(8,128)(4,1)S(1)}, pred[80,1408]{1,0:T(8,128)(4,1)}, u32[]{:S(2)}) copy-start(pred[80,1408]{1,0:T(8,128)(4,1)} %copy-done.9) | copy-start | bytes 337924
  401.1 41.6 %copy-start.1 = (bf16[192,512]{1,0:T(8,128)(2,1)S(1)}, bf16[192,512]{1,0:T(8,128)(2,1)}, u32[]{:S(2)}) copy-start(bf16[192,512]{1,0:T(8,128)(2,1)} %param.11) | copy-start | bytes 589828
Sparse Core Ops, SparseCore 0:
  317.8 35.1 all-reduce.8
  359.5 79.5 all-reduce.6
